TPU v7x, 32 devices: a whole 2x2x4 slice. The times are simulated.
32 devices in a mesh: dp: 16 (over z, x, core), mp: 2 (over y).
Axes of the slice: x: 2, y: 2, z: 4, core: 2. Of those that a mesh axis runs over, the one named last changes fastest.
Arguments:
- layer_in: bfloat16 [4096, 2048], P('dp'), may hold values from -6 to 6
- out_grad: bfloat16 [4096, 2048], P('dp'), may hold values from -6 to 6
- norm_gain: bfloat16 [2, 2048], P(None, 'dp'), may hold values from 0.5 to 1.5
- norm_bias: bfloat16 [2, 2048], P(None, 'dp'), may hold values from -1.5 to 1.5
- qkv_weight: bfloat16 [3, 2048, 2048], P(None, 'dp', 'mp'), may hold values from -0.125 to 0.125
- qkv_bias: bfloat16 [3, 8, 256], P(None, 'mp', 'dp'), may hold values from -12 to 12
- out_weight: bfloat16 [2048, 2048], P('mp', 'dp'), may hold values from -1 to 1
- attn_bias: bfloat16 [2048], P('dp'), may hold values from -1.5 to 1.5
- up_weight: bfloat16 [2048, 8192], P('dp', 'mp'), may hold values from -0.125 to 0.125
- up_bias: bfloat16 [64, 128], P('mp', 'dp'), may hold values from -1.5 to 1.5
- down_weight: bfloat16 [8192, 2048], P('mp', 'dp'), may hold values from -0.0625 to 0.0625
- mlp_bias: bfloat16 [2048], P('dp'), may hold values from -1.5 to 1.5
Outputs:
- layer_out: float32 [4096, 2048], P('dp')
- in_grad: float32 [4096, 2048], P('dp')
- gain_grad: float32 [2, 2048], P(None, 'dp')
- shift_grad: float32 [2, 2048], P(None, 'dp')
- qkv_grad: float32 [3, 2048, 2048], P(None, 'dp', 'mp')
- qkv_bias_grad: float32 [3, 8, 256], P(None, 'mp', 'dp')
- out_weight_grad: float32 [2048, 2048], P('mp', 'dp')
- out_bias_grad: float32 [2048], P('dp')
- up_grad: float32 [2048, 8192], P('dp', 'mp')
- up_bias_grad: float32 [64, 128], P('mp', 'dp')
- down_grad: float32 [8192, 2048], P('mp', 'dp')
All inputs are finite; a program needn't handle non-finite values.
Results may differ from a plain program's by a relative error of at most 0.0095.
The roundings to bfloat16 on the way count: a program that leaves them out, or rounds other values in their place, can miss the bound.
Values may be sent and summed in bfloat16 or wider, within the bound.
No kernel may reach another device: no remote copies, remote signals or barrier semaphores. Data moves between devices by JAX's collectives and lax.ppermute only.
A program may use at most 256 MiB of HBM per device.

v0:
```python
import math
import jax
import jax.numpy as jnp
from jax import lax
from jax.sharding import PartitionSpec as P

HEAD = 256
ROT = 64
SEQ = 256
EPS = 1e-05
NORMAL_PEAK = 0.3989422804014327
ROOT_HALF = 0.7071067811865476


def normalize(rows_in):
    mean_row = jnp.mean(rows_in, axis=-1, keepdims=True)
    centred = rows_in - mean_row
    variance = jnp.mean(centred * centred, axis=-1, keepdims=True)
    inv_std = lax.rsqrt(variance + EPS)
    return (centred * inv_std, inv_std)


def rotary(length, half_rot, full_rot):
    position = jnp.arange(length, dtype=jnp.float32)[:, None]
    exponent = jnp.arange(half_rot, dtype=jnp.float32) * (2.0 / full_rot)
    angle = position * jnp.exp(-math.log(10000.0) * exponent)[None, :]
    return (jnp.cos(angle), jnp.sin(angle))


def turn(tensor, cosine, sine, sign):
    half_rot = cosine.shape[-1]
    lead_part = tensor[..., :half_rot]
    next_part = tensor[..., half_rot : 2 * half_rot]
    rest_part = tensor[..., 2 * half_rot :]
    cos_rows = cosine[None, :, None, :]
    sin_rows = sign * sine[None, :, None, :]
    return jnp.concatenate(
        [
            lead_part * cos_rows - next_part * sin_rows,
            next_part * cos_rows + lead_part * sin_rows,
            rest_part,
        ],
        axis=-1,
    )


def causal_scores(queries, keys_rot):
    scale = HEAD ** (-0.5)
    scores = (
        jnp.einsum("bqhe,bkhe->bhqk", queries, keys_rot, preferred_element_type=jnp.float32) * scale
    )
    length = scores.shape[-1]
    causal = lax.broadcasted_iota(jnp.int32, (length, length), 0) >= lax.broadcasted_iota(
        jnp.int32, (length, length), 1
    )
    return jnp.where(causal, scores, -jnp.inf)


def attend(queries, keys_rot, values):
    scores = causal_scores(queries, keys_rot)
    top_score = jnp.max(scores, axis=-1, keepdims=True)
    total = jnp.sum(jnp.exp(scores - top_score), axis=-1, keepdims=True)
    log_total = top_score + jnp.log(total)
    probs = jnp.exp(scores - log_total).astype(jnp.bfloat16)
    context = jnp.einsum("bhqk,bkhe->bqhe", probs, values, preferred_element_type=jnp.float32)
    return (context.astype(jnp.bfloat16), log_total)


def attend_back(queries, keys_rot, values, log_total, grad_context):
    scale = HEAD ** (-0.5)
    prob_full = jnp.exp(causal_scores(queries, keys_rot) - log_total)
    probs = prob_full.astype(jnp.bfloat16)
    grad_values = jnp.einsum(
        "bhqk,bqhe->bkhe", probs, grad_context, preferred_element_type=jnp.float32
    )
    grad_probs = jnp.einsum(
        "bqhe,bkhe->bhqk", grad_context, values, preferred_element_type=jnp.float32
    )
    grad_scores = prob_full * (grad_probs - jnp.sum(prob_full * grad_probs, axis=-1, keepdims=True))
    scores_half = grad_scores.astype(jnp.bfloat16)
    grad_queries = (
        jnp.einsum("bhqk,bkhe->bqhe", scores_half, keys_rot, preferred_element_type=jnp.float32)
        * scale
    )
    grad_keys = (
        jnp.einsum("bhqk,bqhe->bkhe", scores_half, queries, preferred_element_type=jnp.float32)
        * scale
    )
    return (grad_queries, grad_keys, grad_values)


def gelu_slope(value):
    return (
        0.5 * (1.0 + lax.erf(value * ROOT_HALF))
        + value * jnp.exp(-0.5 * value * value) * NORMAL_PEAK
    )


def contract(left, right):
    return lax.dot_general(
        left, right, (((0,), (0,)), ((), ())), preferred_element_type=jnp.float32
    )


def project_back(left, right):
    return lax.dot_general(
        left, right, (((1,), (1,)), ((), ())), preferred_element_type=jnp.float32
    )


def on_device(
    layer_in,
    out_grad,
    norm_gain,
    norm_bias,
    qkv_weight,
    qkv_bias,
    out_weight,
    attn_bias,
    up_weight,
    up_bias,
    down_weight,
    mlp_bias,
):
    (
        gain_all,
        shift_all,
        qkv_all,
        qkv_shift,
        out_all,
        attn_shift,
        up_all,
        up_shift,
        down_all,
        mlp_shift,
    ) = (
        lax.all_gather(norm_gain, "dp", axis=1, tiled=True),
        lax.all_gather(norm_bias, "dp", axis=1, tiled=True),
        lax.all_gather(qkv_weight, "dp", axis=1, tiled=True),
        lax.all_gather(qkv_bias, "dp", axis=2, tiled=True),
        lax.all_gather(out_weight, "dp", axis=1, tiled=True),
        lax.all_gather(attn_bias, "dp", axis=0, tiled=True),
        lax.all_gather(up_weight, "dp", axis=0, tiled=True),
        lax.all_gather(up_bias, "dp", axis=1, tiled=True),
        lax.all_gather(down_weight, "dp", axis=1, tiled=True),
        lax.all_gather(mlp_bias, "dp", axis=0, tiled=True),
    )
    row_count = layer_in.shape[0]
    seq_count = row_count // SEQ
    head_count = qkv_shift.shape[1]
    local_width = qkv_all.shape[2]
    inputs = layer_in.astype(jnp.float32)
    unit_rows, inv_std = normalize(inputs)
    gains = gain_all.astype(jnp.float32)
    shifts = shift_all.astype(jnp.float32)
    normed_attn = (unit_rows * gains[0] + shifts[0]).astype(jnp.bfloat16)
    normed_mlp = (unit_rows * gains[1] + shifts[1]).astype(jnp.bfloat16)
    cosine, sine = rotary(SEQ, ROT // 2, ROT)
    projected = [
        jnp.dot(normed_attn, qkv_all[index], preferred_element_type=jnp.float32)
        + qkv_shift[index].reshape(local_width).astype(jnp.float32)
        for index in range(3)
    ]
    shaped = [item.reshape(seq_count, SEQ, head_count, HEAD) for item in projected]
    queries = turn(shaped[0], cosine, sine, 1.0).astype(jnp.bfloat16)
    keys_rot = turn(shaped[1], cosine, sine, 1.0).astype(jnp.bfloat16)
    values = shaped[2].astype(jnp.bfloat16)
    context, log_total = attend(queries, keys_rot, values)
    context_rows = context.reshape(row_count, local_width)
    pre_act = jnp.dot(normed_mlp, up_all, preferred_element_type=jnp.float32) + up_shift.reshape(
        -1
    ).astype(jnp.float32)
    activated = jax.nn.gelu(pre_act, approximate=False).astype(jnp.bfloat16)
    branch_sum = jnp.dot(context_rows, out_all, preferred_element_type=jnp.float32) + jnp.dot(
        activated, down_all, preferred_element_type=jnp.float32
    )
    mixed = lax.psum(branch_sum.astype(jnp.bfloat16), "mp").astype(jnp.float32)
    layer_out = inputs + mixed + attn_shift.astype(jnp.float32) + mlp_shift.astype(jnp.float32)
    gain_back, qkv_back, out_back, up_back, down_back = (
        lax.all_gather(norm_gain, "dp", axis=1, tiled=True),
        lax.all_gather(qkv_weight, "dp", axis=1, tiled=True),
        lax.all_gather(out_weight, "dp", axis=1, tiled=True),
        lax.all_gather(up_weight, "dp", axis=0, tiled=True),
        lax.all_gather(down_weight, "dp", axis=1, tiled=True),
    )
    out_bias_grad = jnp.sum(out_grad.astype(jnp.float32), axis=0)
    down_grad = contract(activated, out_grad)
    grad_act = project_back(out_grad, down_back)
    grad_pre = grad_act * gelu_slope(pre_act)
    up_bias_grad = jnp.sum(grad_pre, axis=0).reshape(up_shift.shape)
    pre_half = grad_pre.astype(jnp.bfloat16)
    up_grad = contract(normed_mlp, pre_half)
    grad_normed_mlp = project_back(pre_half, up_back)
    out_weight_grad = contract(context_rows, out_grad)
    grad_context = (
        project_back(out_grad, out_back)
        .astype(jnp.bfloat16)
        .reshape(seq_count, SEQ, head_count, HEAD)
    )
    grad_queries, grad_keys, grad_values = attend_back(
        queries, keys_rot, values, log_total, grad_context
    )
    grad_proj = [
        turn(grad_queries, cosine, sine, -1.0).reshape(row_count, local_width),
        turn(grad_keys, cosine, sine, -1.0).reshape(row_count, local_width),
        grad_values.reshape(row_count, local_width),
    ]
    qkv_bias_grad = jnp.stack([jnp.sum(item, axis=0) for item in grad_proj]).reshape(
        3, head_count, HEAD
    )
    proj_half = [item.astype(jnp.bfloat16) for item in grad_proj]
    qkv_grad = jnp.stack([contract(normed_attn, item) for item in proj_half])
    grad_normed_attn = project_back(proj_half[0], qkv_back[0])
    grad_normed_attn = grad_normed_attn + project_back(proj_half[1], qkv_back[1])
    grad_normed_attn = grad_normed_attn + project_back(proj_half[2], qkv_back[2])
    summed_attn, summed_mlp = (
        lax.psum(grad_normed_attn.astype(jnp.bfloat16), "mp").astype(jnp.float32),
        lax.psum(grad_normed_mlp.astype(jnp.bfloat16), "mp").astype(jnp.float32),
    )
    gain_grad = jnp.stack(
        [jnp.sum(summed_attn * unit_rows, axis=0), jnp.sum(summed_mlp * unit_rows, axis=0)]
    )
    shift_grad = jnp.stack([jnp.sum(summed_attn, axis=0), jnp.sum(summed_mlp, axis=0)])
    back_gains = gain_back.astype(jnp.float32)
    grad_unit = summed_attn * back_gains[0] + summed_mlp * back_gains[1]
    in_grad = out_grad.astype(jnp.float32) + inv_std * (
        grad_unit
        - jnp.mean(grad_unit, axis=-1, keepdims=True)
        - unit_rows * jnp.mean(grad_unit * unit_rows, axis=-1, keepdims=True)
    )
    (
        gain_out,
        shift_out,
        qkv_out,
        qkv_bias_out,
        out_weight_out,
        out_bias_out,
        up_out,
        up_bias_out,
        down_out,
    ) = (
        lax.psum_scatter(gain_grad, "dp", scatter_dimension=1, tiled=True),
        lax.psum_scatter(shift_grad, "dp", scatter_dimension=1, tiled=True),
        lax.psum_scatter(qkv_grad, "dp", scatter_dimension=1, tiled=True),
        lax.psum_scatter(qkv_bias_grad, "dp", scatter_dimension=2, tiled=True),
        lax.psum_scatter(out_weight_grad, "dp", scatter_dimension=1, tiled=True),
        lax.psum_scatter(out_bias_grad, "dp", scatter_dimension=0, tiled=True),
        lax.psum_scatter(up_grad, "dp", scatter_dimension=0, tiled=True),
        lax.psum_scatter(up_bias_grad, "dp", scatter_dimension=1, tiled=True),
        lax.psum_scatter(down_grad, "dp", scatter_dimension=1, tiled=True),
    )
    return (
        layer_out,
        in_grad,
        gain_out,
        shift_out,
        qkv_out,
        qkv_bias_out,
        out_weight_out,
        out_bias_out,
        up_out,
        up_bias_out,
        down_out,
    )


def solution(mesh):
    placed = (
        P("dp", None),
        P("dp", None),
        P(None, "dp"),
        P(None, "dp"),
        P(None, "dp", "mp"),
        P(None, "mp", "dp"),
        P("mp", "dp"),
        P("dp"),
        P("dp", "mp"),
        P("mp", "dp"),
        P("mp", "dp"),
        P("dp"),
    )
    return jax.shard_map(
        on_device,
        mesh=mesh,
        in_specs=placed,
        out_specs=(
            P("dp", None),
            P("dp", None),
            P(None, "dp"),
            P(None, "dp"),
            P(None, "dp", "mp"),
            P(None, "mp", "dp"),
            P("mp", "dp"),
            P("dp"),
            P("dp", "mp"),
            P("mp", "dp"),
            P("mp", "dp"),
        ),
        check_vma=False,
    )
```

profile of v0, /device:TPU:0, one launch (start us, length us, event | category | flops | bytes accessed | tf_op | source)
XLA Modules:
  0.0 1756.7 jit_solution(10714257107157818907)
XLA Ops:
  10.9 23.5 %all_gather.41 = bf16[32,128]{0,1:T(8,128)(2,1)S(1)} all-gather(bf16[32,8]{0,1:T(8,128)(2,1)} %param.21), channel_id=1, replica_groups=mesh['dp'=16,'mp'=2] {'dp'}, dimensions={1}, use_global_device_ids=true | all-gather | bytes 8704 | tf_op jit(solution)/shard_map/all_gather | solution.py:144
  34.4 19.0 %all_gather.38 = bf16[3,4,256]{1,0,2:T(4,128)(2,1)S(1)} all-gather(bf16[3,4,16]{1,0,2:T(4,128)(2,1)S(1)} %copy.112), channel_id=1, replica_groups=mesh['dp'=16,'mp'=2] {'dp'}, dimensions={2}, use_global_device_ids=true | all-gather | bytes 6528 | tf_op jit(solution)/shard_map/all_gather | solution.py:140
  55.3 19.7 %all_gather.35 = bf16[2,2048]{1,0:T(2,128)(2,1)S(1)} all-gather(bf16[2,128]{1,0:T(2,128)(2,1)S(1)} %copy-done.29), channel_id=1, replica_groups=mesh['dp'=16,'mp'=2] {'dp'}, dimensions={1}, use_global_device_ids=true | all-gather | bytes 8704 | tf_op jit(solution)/shard_map/all_gather | solution.py:137
  75.0 18.0 %all_gather.36 = bf16[2,2048]{1,0:T(2,128)(2,1)S(1)} all-gather(bf16[2,128]{1,0:T(2,128)(2,1)S(1)} %copy-done.30), channel_id=1, replica_groups=mesh['dp'=16,'mp'=2] {'dp'}, dimensions={1}, use_global_device_ids=true | all-gather | bytes 8704 | tf_op jit(solution)/shard_map/all_gather | solution.py:138
  101.1 66.4 %all-gather.7.cloned.1.call-done = bf16[3,2048,1024]{2,1,0:T(8,128)(2,1)} async-done(((bf16[3,128,1024]{2,1,0:T(8,128)(2,1)}), bf16[3,2048,1024]{2,1,0:T(8,128)(2,1)}) %all-gather.7.cloned.1.call-update) | async-done | bytes 12582928 | tf_op jit(solution)/shard_map/all_gather | solution.py:139
  167.5 4.5 fusion.47
  174.8 5.0 fusion.48
  188.7 3.5 fusion.50
  210.4 3.7 fusion.16
  214.1 3.5 fusion.20
  217.7 5.2 fusion.23
  222.9 71.5 %all-gather.11.cloned.1.call-done = bf16[2048,4096]{1,0:T(8,128)(2,1)} async-done(((bf16[128,4096]{1,0:T(8,128)(2,1)}), bf16[2048,4096]{1,0:T(8,128)(2,1)}) %all-gather.11.cloned.1.call-update) | async-done | bytes 16777232 | tf_op jit(solution)/shard_map/all_gather | solution.py:143
  294.4 19.0 %fusion.2 = (bf16[256,4096]{1,0:T(8,128)(2,1)}, f32[256,4096]{1,0:T(8,128)}) fusion(f32[4096]{0:T(1024)S(1)} %copy-done.27, bf16[2048,4096]{1,0:T(8,128)(2,1)} %all-gather.11.cloned.1.call-done, bf16[256,2048]{1,0:T(8,128)(2,1)S(1)} %copy-done, f32[2048]{0:T(1024)S(1)} %bitcast.169, f32[2048]{0:T(1024)S(1)} %bitcast.165, f32[256]{0:T(256)S(1)} %copy-done.24, ...), kind=kOutput, calls=%fused_computation.10 | convolution fusion | flops 4367319040 | bytes 24152064 | tf_op jit(solution)/shard_map/dot_general | solution.py:170
  313.5 111.0 %all-gather.13.cloned.1.call-done = bf16[4096,2048]{1,0:T(8,128)(2,1)} async-done(((bf16[4096,128]{1,0:T(8,128)(2,1)}), bf16[4096,2048]{1,0:T(8,128)(2,1)}) %all-gather.13.cloned.1.call-update) | async-done | bytes 16777232 | tf_op jit(solution)/shard_map/all_gather | solution.py:145
  424.5 11.0 fusion.89
  435.5 9.6 fusion.90
  445.1 11.9 convolution_convert_fusion
  457.0 5.1 fusion.22
  467.5 78.9 %all-reduce.6.cloned.1.call-done = (bf16[256,2048]{1,0:T(8,128)(2,1)}, bf16[256,2048]{1,0:T(8,128)(2,1)}, bf16[256,2048]{1,0:T(8,128)(2,1)}) async-done(((bf16[256,2048]{1,0:T(8,128)(2,1)}, bf16[256,2048]{1,0:T(8,128)(2,1)}, bf16[256,2048]{1,0:T(8,128)(2,1)}), (bf16[256,2048]{1,0:T(8,128)(2,1)}, bf16[256,2048]{1,0:T(8,128)(2,1)}, bf16[256,2048]{1,0:T(8,128)(2,1)})) %all-reduce.6.cloned.1.call-update) | async-done | bytes 3145744 | tf_op jit(solution)/shard_map/psum | solution.py:177
  552.4 4.6 fusion.91
  562.4 8.7 pad_maximum_fusion
  571.2 14.9 fusion.51
  586.2 14.8 fusion.92
  603.5 21.4 %all-gather = bf16[16,1,128]{2,1,0:T(2,128)(2,1)S(1)} all-gather(bf16[1,1,128]{2,1,0:T(2,128)(2,1)S(1)} %bitcast.187), channel_id=1, replica_groups=mesh['dp'=16,'mp'=2] {'dp'}, dimensions={0}, use_global_device_ids=true | all-gather | bytes 4352 | tf_op jit(solution)/shard_map/all_gather | solution.py:142
  624.9 17.4 all-gather.1
  643.9 5.3 convert_reduce_fusion.3
  649.2 59.1 %all-reduce.2 = (f32[2048]{0:T(1024)S(1)}, f32[32,128]{1,0:T(8,128)S(1)}) all-reduce(f32[2048]{0:T(1024)S(1)} %get-tuple-element.74, f32[32,128]{1,0:T(8,128)S(1)} %bitcast.183), channel_id=7, replica_groups=mesh['dp'=16,'mp'=2] {'dp'}, use_global_device_ids=true, to_apply=%region_23.24.clone | all-reduce | flops 6144 | bytes 49152
  711.1 14.9 reduce-scatter.23.cloned.1.call-done
  727.5 105.8 %reduce-scatter.17.cloned.1.call-done = f32[1024,128]{1,0:T(8,128)} async-done(((f32[1024,2048]{1,0:T(8,128)}), f32[1024,128]{1,0:T(8,128)}) %reduce-scatter.17.cloned.1.call-update) | async-done | bytes 524304 | tf_op jit(solution)/shard_map/reduce_scatter | solution.py:246
  833.3 247.5 %reduce-scatter.15.cloned.1.call-done = f32[3,128,1024]{2,1,0:T(8,128)} async-done(((f32[3,2048,1024]{2,1,0:T(8,128)}), f32[3,128,1024]{2,1,0:T(8,128)}) %reduce-scatter.15.cloned.1.call-update) | async-done | bytes 1572880 | tf_op jit(solution)/shard_map/reduce_scatter | solution.py:244
  1080.8 334.5 %reduce-scatter.19.cloned.1.call-done = f32[128,4096]{1,0:T(8,128)} async-done(((f32[2048,4096]{1,0:T(8,128)}), f32[128,4096]{1,0:T(8,128)}) %reduce-scatter.19.cloned.1.call-update) | async-done | bytes 2097168 | tf_op jit(solution)/shard_map/reduce_scatter | solution.py:248
  1415.3 334.1 %reduce-scatter.21.cloned.1.call-done = f32[4096,128]{1,0:T(8,128)} async-done(((f32[4096,2048]{1,0:T(8,128)}), f32[4096,128]{1,0:T(8,128)}) %reduce-scatter.21.cloned.1.call-update) | async-done | bytes 2097168 | tf_op jit(solution)/shard_map/reduce_scatter | solution.py:250
  (167 shorter events, 67.1 us)
Async XLA Ops:
  7.2 48.1 %copy-start.29 = (bf16[2,128]{1,0:T(2,128)(2,1)S(1)}, bf16[2,128]{1,0:T(2,128)(2,1)}, u32[]{:S(2)}) copy-start(bf16[2,128]{1,0:T(2,128)(2,1)} %param.14) | copy-start | bytes 1540
  7.2 67.8 %copy-start.30 = (bf16[2,128]{1,0:T(2,128)(2,1)S(1)}, bf16[2,128]{1,0:T(2,128)(2,1)}, u32[]{:S(2)}) copy-start(bf16[2,128]{1,0:T(2,128)(2,1)} %param.15) | copy-start | bytes 1540
  7.2 86.4 %copy-start = (bf16[256,2048]{1,0:T(8,128)(2,1)S(1)}, bf16[256,2048]{1,0:T(8,128)(2,1)}, u32[]{:S(2)}) copy-start(bf16[256,2048]{1,0:T(8,128)(2,1)} %param.12) | copy-start | bytes 3145732
  7.2 89.4 %copy-start.1 = (bf16[256,2048]{1,0:T(8,128)(2,1)S(1)}, bf16[256,2048]{1,0:T(8,128)(2,1)}, u32[]{:S(2)}) copy-start(bf16[256,2048]{1,0:T(8,128)(2,1)} %param.13) | copy-start | bytes 3145732
  7.2 89.4 %all-gather.9.cloned.1.call-start = ((), (), s32[]{:S(2)}) async-start(), calls=%async_computation.8 | async-start | bytes 4456448 | tf_op jit(solution)/shard_map/all_gather | solution.py:141
  8.0 159.6 %all-gather.7.cloned.1.call-start = ((), (), s32[]{:S(2)}) async-start(), calls=%async_computation.7 | async-start | bytes 13369344 | tf_op jit(solution)/shard_map/all_gather | solution.py:139
  8.7 285.7 %all-gather.11.cloned.1.call-start = ((), (), s32[]{:S(2)}) async-start(), calls=%async_computation.9 | async-start | bytes 17825792 | tf_op jit(solution)/shard_map/all_gather | solution.py:143
  9.4 415.1 %all-gather.13.cloned.1.call-start = ((), (), s32[]{:S(2)}) async-start(), calls=%async_computation.10 | async-start | bytes 17825792 | tf_op jit(solution)/shard_map/all_gather | solution.py:145
  10.0 536.3 %all-reduce.6.cloned.1.call-start = ((), (), s32[]{:S(2)}) async-start(), calls=%async_computation.18 | async-start | bytes 6291456 | tf_op jit(solution)/shard_map/psum | solution.py:177
  93.9 73.7 %copy-start.19 = (f32[256]{0:T(256)}, f32[256]{0:T(256)S(1)}, u32[]{:S(2)}) copy-start(f32[256]{0:T(256)S(1)} %broadcast_multiply_fusion.3) | copy-start | bytes 3076
  94.3 73.2 %copy-start.22 = (f32[256]{0:T(256)}, f32[256]{0:T(256)S(1)}, u32[]{:S(2)}) copy-start(f32[256]{0:T(256)S(1)} %add_rsqrt_fusion) | copy-start | bytes 3076
  188.7 3.6 copy-start.8
  206.5 3.8 copy-start.13
  210.3 7.3 copy-start.15
  210.3 3.7 copy-start.4
  217.6 76.8 %copy-start.18 = (f32[1,2048]{1,0:T(1,128)S(1)}, f32[1,2048]{1,0:T(1,128)}, u32[]{:S(2)}) copy-start(f32[1,2048]{1,0:T(1,128)} %get-tuple-element.91) | copy-start | bytes 24580
  217.6 76.8 %copy-start.21 = (f32[256]{0:T(256)S(1)}, f32[256]{0:T(256)}, u32[]{:S(2)}) copy-start(f32[256]{0:T(256)} %copy-done.19) | copy-start | bytes 3076
  217.6 76.8 %copy-start.24 = (f32[256]{0:T(256)S(1)}, f32[256]{0:T(256)}, u32[]{:S(2)}) copy-start(f32[256]{0:T(256)} %copy-done.22) | copy-start | bytes 3076
  217.6 76.8 %copy-start.25 = (f32[1,2048]{1,0:T(1,128)S(1)}, f32[1,2048]{1,0:T(1,128)}, u32[]{:S(2)}) copy-start(f32[1,2048]{1,0:T(1,128)} %get-tuple-element.93) | copy-start | bytes 24580
  217.7 76.8 %copy-start.27 = (f32[4096]{0:T(1024)S(1)}, f32[4096]{0:T(1024)}, u32[]{:S(2)}) copy-start(f32[4096]{0:T(1024)} %bitcast_convert_fusion) | copy-start | bytes 49156
  424.5 11.0 copy-start.10
  445.1 12.0 copy-start.11
  462.1 180.2 %reduce-scatter.27.cloned.1.call-start = ((), (), s32[]{:S(2)}) async-start(), calls=%async_computation.17 | async-start | bytes 139264
  466.5 85.9 %copy-start.12 = (bf16[4,256,256]{2,1,0:T(8,128)(2,1)S(1)}, bf16[4,256,256]{2,1,0:T(8,128)(2,1)}, u32[]{:S(2)}) copy-start(bf16[4,256,256]{2,1,0:T(8,128)(2,1)} %convolution_convert_fusion.1) | copy-start | bytes 1572868
  467.4 242.2 %reduce-scatter.25.cloned.1.call-start = ((), (), s32[]{:S(2)}) async-start(), calls=%async_computation.16 | async-start | bytes 1114112
  550.9 175.1 %reduce-scatter.23.cloned.1.call-start = ((), (), s32[]{:S(2)}) async-start(), calls=%async_computation.15 | async-start | bytes 1114112
  552.4 281.0 %reduce-scatter.17.cloned.1.call-start = ((), (), s32[]{:S(2)}) async-start(), calls=%async_computation.12 | async-start | bytes 8912896 | tf_op jit(solution)/shard_map/reduce_scatter | solution.py:246
  557.0 523.8 %reduce-scatter.15.cloned.1.call-start = ((), (), s32[]{:S(2)}) async-start(), calls=%async_computation.11 | async-start | bytes 26738688 | tf_op jit(solution)/shard_map/reduce_scatter | solution.py:244
  571.1 844.2 %reduce-scatter.19.cloned.1.call-start = ((), (), s32[]{:S(2)}) async-start(), calls=%async_computation.13 | async-start | bytes 35651584 | tf_op jit(solution)/shard_map/reduce_scatter | solution.py:248
  586.1 1163.3 %reduce-scatter.21.cloned.1.call-start = ((), (), s32[]{:S(2)}) async-start(), calls=%async_computation.14 | async-start | bytes 35651584 | tf_op jit(solution)/shard_map/reduce_scatter | solution.py:250
  601.0 23.9 %copy-start.32 = (bf16[128]{0:T(256)(128)(2,1)S(1)}, bf16[128]{0:T(256)(128)(2,1)}, u32[]{:S(2)}) copy-start(bf16[128]{0:T(256)(128)(2,1)} %param.23) | copy-start | bytes 772
  601.0 42.9 %copy-start.9 = (bf16[256,2048]{1,0:T(8,128)(2,1)S(1)}, bf16[256,2048]{1,0:T(8,128)(2,1)}, u32[]{:S(2)}) copy-start(bf16[256,2048]{1,0:T(8,128)(2,1)} %get-tuple-element.64) | copy-start | bytes 3145732
  (14 other events, 21.6 us)
Sparse Core Ops, SparseCore 0:
  10.2 56.1 all-gather.8
  68.6 98.8 all-gather.6
  169.7 124.6 all-gather.10
  296.4 128.0 all-gather.12
  462.3 84.0 all-reduce.5
  549.7 55.5 reduce-scatter.26
  608.9 56.6 reduce-scatter.24
  669.2 56.7 reduce-scatter.22
  730.7 102.6 reduce-scatter.16
  837.9 242.9 reduce-scatter.14
  1085.7 329.5 reduce-scatter.18
  1420.0 329.4 reduce-scatter.20
where the time goes:
time: 1770 us; the launch traced here: 1760 us
  waiting for transfers between devices  1370 us (77%)
  blocking collectives  178 us (10%)
  matrix products  131 us (7%)
  local copies, waits for them, and re-layouts  33.6 us (2%)
  other arithmetic  29.5 us (2%)
    reduce_scatter x1, waiting for transfers between devices, on_device(): lax.psum_scatter(up_grad, 'dp', scatter_dimension=0, tiled=True)  334 us
    reduce_scatter x1, waiting for transfers between devices, on_device(): lax.psum_scatter(down_grad, 'dp', scatter_dimension=1, tiled=True)  334 us
    reduce_scatter x1, waiting for transfers between devices, on_device(): lax.psum_scatter(qkv_grad, 'dp', scatter_dimension=1, tiled=True)  247 us
    all_gather x1, waiting for transfers between devices, on_device(): lax.all_gather(down_weight, 'dp', axis=1, tiled=True)  111 us
    reduce_scatter x1, waiting for transfers between devices, on_device(): lax.psum_scatter(out_weight_grad, 'dp', scatter_dimension=1, tiled=True)  106 us
    psum x1, waiting for transfers between devices, on_device(): mixed = lax.psum(branch_sum.astype(jnp.bfloat16), 'mp').astype(jnp.float32)  78.9 us
    all_gather x1, waiting for transfers between devices, on_device(): lax.all_gather(up_weight, 'dp', axis=0, tiled=True)  71.5 us
    all_gather x1, waiting for transfers between devices, on_device(): lax.all_gather(qkv_weight, 'dp', axis=1, tiled=True)  66.4 us
  transfers between devices with their start and end apart: 12, of which 9 were waited for; matrix products, arithmetic and copies ran while one was open for 9% of the time, Pallas kernels for 0%

commit v1 on v0

--- a/solution.py
+++ b/solution.py
@@ -10,6 +10,27 @@
 EPS = 1e-05
 NORMAL_PEAK = 0.3989422804014327
 ROOT_HALF = 0.7071067811865476
+
+
+def collect(shard, axis, dim):
+    peers, mine, span = (lax.axis_size(axis), lax.axis_index(axis), shard.shape[dim])
+    right = [(i, (i + 1) % peers) for i in range(peers)]
+    left = [(i, (i - 1) % peers) for i in range(peers)]
+    result = jnp.zeros((*shard.shape[:dim], peers * span, *shard.shape[dim + 1 :]), shard.dtype)
+    result = lax.dynamic_update_slice_in_dim(result, shard, mine * span, axis=dim)
+    from_left = from_right = shard
+    half = peers // 2
+    for step in range(1, half + 1):
+        from_left = lax.ppermute(from_left, axis, right)
+        result = lax.dynamic_update_slice_in_dim(
+            result, from_left, (mine - step) % peers * span, axis=dim
+        )
+        if step < peers - half:
+            from_right = lax.ppermute(from_right, axis, left)
+            result = lax.dynamic_update_slice_in_dim(
+                result, from_right, (mine + step) % peers * span, axis=dim
+            )
+    return result
 
 
 def normalize(rows_in):
@@ -142,7 +163,7 @@
         lax.all_gather(attn_bias, "dp", axis=0, tiled=True),
         lax.all_gather(up_weight, "dp", axis=0, tiled=True),
         lax.all_gather(up_bias, "dp", axis=1, tiled=True),
-        lax.all_gather(down_weight, "dp", axis=1, tiled=True),
+        collect(down_weight, "dp", 1),
         lax.all_gather(mlp_bias, "dp", axis=0, tiled=True),
     )
     row_count = layer_in.shape[0]

time: 1770 us -> 1840 us (1.040)
  blocking collectives: 178 us -> 240 us
  waiting for transfers between devices: 1370 us -> 1320 us
  local copies, waits for them, and re-layouts: 33.6 us -> 65.6 us
  starting transfers between devices: 0.7 us -> 26.2 us
    ppermute x0 -> x15, waiting for transfers between devices: none -> 113 us  [the longest x7 99 us: collect(): from_right = lax.ppermute(from_right, axis, left)]
    all_gather x1, waiting for transfers between devices: 71.5 us -> 0.01 us  [on_device(): lax.all_gather(up_weight, 'dp', axis=0, tiled=True)]
    all_gather x1, waiting for transfers between devices: 66.4 us -> 0.01 us  [on_device(): lax.all_gather(qkv_weight, 'dp', axis=1, tiled=True)]
    all_gather x1, blocking collectives: 18 us -> 52.2 us  [on_device(): lax.all_gather(norm_bias, 'dp', axis=1, tiled=True)]
    ppermute x0 -> x15, starting transfers between devices: none -> 25.5 us  [the longest x7 23.8 us: collect(): from_right = lax.ppermute(from_right, axis, left)]
    dynamic_update_slice x0 -> x16, local copies, waits for them, and re-layouts: none -> 23.1 us  [the longest x8 12.7 us: collect(): lax.dynamic_update_slice_in_dim(result, from_left, (mine - step) % peers...]
    all_gather x1, waiting for transfers between devices: 111 us -> 89.1 us  [on_device(): lax.all_gather(down_weight, 'dp', axis=1, tiled=True)]
  transfers between devices with their start and end apart: 12 -> 27, of which waited for: 9 -> 15; matrix products, arithmetic and copies ran while one was open for 9% -> 11% of each run, Pallas kernels for 0% -> 0%
where the time goes in v1:
time: 1840 us; the launch traced here: 1830 us
  waiting for transfers between devices  1320 us (72%)
  blocking collectives  240 us (13%)
  matrix products  127 us (7%)
  local copies, waits for them, and re-layouts  65.6 us (4%)
  other arithmetic  32.3 us (2%)
  starting transfers between devices  26.2 us (1%)
    reduce_scatter x1, waiting for transfers between devices, on_device(): lax.psum_scatter(up_grad, 'dp', scatter_dimension=0, tiled=True)  334 us
    reduce_scatter x1, waiting for transfers between devices, on_device(): lax.psum_scatter(down_grad, 'dp', scatter_dimension=1, tiled=True)  334 us
    reduce_scatter x1, waiting for transfers between devices, on_device(): lax.psum_scatter(qkv_grad, 'dp', scatter_dimension=1, tiled=True)  248 us
    reduce_scatter x1, waiting for transfers between devices, on_device(): lax.psum_scatter(out_weight_grad, 'dp', scatter_dimension=1, tiled=True)  106 us
    ppermute x7, waiting for transfers between devices, collect(): from_right = lax.ppermute(from_right, axis, left)  99 us
    all_gather x1, waiting for transfers between devices, on_device(): lax.all_gather(down_weight, 'dp', axis=1, tiled=True)  89.1 us
    psum x1, waiting for transfers between devices, on_device(): mixed = lax.psum(branch_sum.astype(jnp.bfloat16), 'mp').astype(jnp.float32)  78.9 us
    unnamed x1, blocking collectives  59.1 us
  transfers between devices with their start and end apart: 27, of which 15 were waited for; matrix products, arithmetic and copies ran while one was open for 11% of the time, Pallas kernels for 0%

profile of v1, /device:TPU:0, one launch (start us, length us, event | category | flops | bytes accessed | tf_op | source)
XLA Modules:
  0.0 1829.3 jit_solution(1286113071052956247)
XLA Ops:
  10.6 5.0 collective-permute-start.1
  16.4 37.0 %all_gather.37 = bf16[3,4,256]{1,0,2:T(4,128)(2,1)S(1)} all-gather(bf16[3,4,16]{1,0,2:T(4,128)(2,1)S(1)} %copy.112), channel_id=1, replica_groups=mesh['dp'=16,'mp'=2] {'dp'}, dimensions={2}, use_global_device_ids=true | all-gather | bytes 6528 | tf_op jit(solution)/shard_map/all_gather | solution.py:161
  55.5 20.0 %all_gather.40 = bf16[32,128]{0,1:T(8,128)(2,1)S(1)} all-gather(bf16[32,8]{0,1:T(8,128)(2,1)S(1)} %copy-done.30), channel_id=1, replica_groups=mesh['dp'=16,'mp'=2] {'dp'}, dimensions={1}, use_global_device_ids=true | all-gather | bytes 8704 | tf_op jit(solution)/shard_map/all_gather | solution.py:165
  77.6 33.3 %all_gather.34 = bf16[2,2048]{1,0:T(2,128)(2,1)S(1)} all-gather(bf16[2,128]{1,0:T(2,128)(2,1)S(1)} %copy-done.31), channel_id=1, replica_groups=mesh['dp'=16,'mp'=2] {'dp'}, dimensions={1}, use_global_device_ids=true | all-gather | bytes 8704 | tf_op jit(solution)/shard_map/all_gather | solution.py:158
  117.1 52.2 %all_gather.35 = bf16[2,2048]{1,0:T(2,128)(2,1)S(1)} all-gather(bf16[2,128]{1,0:T(2,128)(2,1)} %param.15), channel_id=1, replica_groups=mesh['dp'=16,'mp'=2] {'dp'}, dimensions={1}, use_global_device_ids=true | all-gather | bytes 8704 | tf_op jit(solution)/shard_map/all_gather | solution.py:159
  170.6 6.0 broadcast_in_dim.12
  179.3 20.1 %collective-permute-done.5 = bf16[4096,128]{1,0:T(8,128)(2,1)S(1)} collective-permute-done((bf16[4096,128]{1,0:T(8,128)(2,1)}, bf16[4096,128]{1,0:T(8,128)(2,1)S(1)}, u32[]{:S(2)}, u32[]{:S(2)}) %collective-permute-start.5) | collective-permute-done | bytes 1048608 | tf_op jit(solution)/shard_map/ppermute | solution.py:29
  209.9 17.4 collective-permute-done.7
  235.4 6.4 collective-permute-done.8
  242.9 17.7 collective-permute-done.9
  270.7 26.0 %collective-permute-done.11 = bf16[4096,128]{1,0:T(8,128)(2,1)S(1)} collective-permute-done((bf16[4096,128]{1,0:T(8,128)(2,1)S(1)}, bf16[4096,128]{1,0:T(8,128)(2,1)S(1)}, u32[]{:S(2)}, u32[]{:S(2)}) %collective-permute-start.11) | collective-permute-done | bytes 1048608 | tf_op jit(solution)/shard_map/ppermute | solution.py:29
  303.6 5.5 collective-permute-done.12
  310.5 17.7 collective-permute-done.13
  388.0 5.0 fusion.23
  393.1 18.4 %fusion.2 = (bf16[256,4096]{1,0:T(8,128)(2,1)S(1)}, f32[256,4096]{1,0:T(8,128)}) fusion(f32[4096]{0:T(1024)S(1)} %copy-done.28, bf16[2048,4096]{1,0:T(8,128)(2,1)} %all-gather.11.cloned.1.call-done, bf16[256,2048]{1,0:T(8,128)(2,1)S(1)} %copy-done, f32[2048]{0:T(1024)S(1)} %bitcast.169, f32[2048]{0:T(1024)S(1)} %bitcast.165, f32[256]{0:T(256)S(1)} %copy-done.25, ...), kind=kOutput, calls=%fused_computation.10 | convolution fusion | flops 4367319040 | bytes 24152064 | tf_op jit(solution)/shard_map/dot_general | solution.py:191
  412.8 9.4 fusion.22
  422.2 89.1 %all-gather.13.cloned.1.call-done = bf16[4096,2048]{1,0:T(8,128)(2,1)} async-done(((bf16[4096,128]{1,0:T(8,128)(2,1)}), bf16[4096,2048]{1,0:T(8,128)(2,1)}) %all-gather.13.cloned.1.call-update) | async-done | bytes 16777232 | tf_op jit(solution)/shard_map/all_gather | solution.py:205
  511.4 11.0 fusion.89
  522.4 12.0 convolution_convert_fusion
  539.6 78.9 %all-reduce.6.cloned.1.call-done = (bf16[256,2048]{1,0:T(8,128)(2,1)}, bf16[256,2048]{1,0:T(8,128)(2,1)}, bf16[256,2048]{1,0:T(8,128)(2,1)}) async-done(((bf16[256,2048]{1,0:T(8,128)(2,1)}, bf16[256,2048]{1,0:T(8,128)(2,1)}, bf16[256,2048]{1,0:T(8,128)(2,1)}), (bf16[256,2048]{1,0:T(8,128)(2,1)}, bf16[256,2048]{1,0:T(8,128)(2,1)}, bf16[256,2048]{1,0:T(8,128)(2,1)})) %all-reduce.6.cloned.1.call-update) | async-done | bytes 3145744 | tf_op jit(solution)/shard_map/psum | solution.py:198
  634.5 8.7 pad_maximum_fusion
  643.3 14.9 fusion.51
  658.3 14.8 fusion.92
  673.8 21.4 %all-gather = bf16[16,1,128]{2,1,0:T(2,128)(2,1)S(1)} all-gather(bf16[1,1,128]{2,1,0:T(2,128)(2,1)S(1)} %bitcast.187), channel_id=1, replica_groups=mesh['dp'=16,'mp'=2] {'dp'}, dimensions={0}, use_global_device_ids=true | all-gather | bytes 4352 | tf_op jit(solution)/shard_map/all_gather | solution.py:163
  695.1 17.5 all-gather.1
  716.0 5.3 convert_reduce_fusion.3
  721.3 59.1 %all-reduce.2 = (f32[2048]{0:T(1024)S(1)}, f32[32,128]{1,0:T(8,128)S(1)}) all-reduce(f32[2048]{0:T(1024)S(1)} %get-tuple-element.74, f32[32,128]{1,0:T(8,128)S(1)} %bitcast.183), channel_id=7, replica_groups=mesh['dp'=16,'mp'=2] {'dp'}, use_global_device_ids=true, to_apply=%region_23.24.clone | all-reduce | flops 6144 | bytes 49152
  783.2 15.6 reduce-scatter.23.cloned.1.call-done
  800.3 105.8 %reduce-scatter.17.cloned.1.call-done = f32[1024,128]{1,0:T(8,128)} async-done(((f32[1024,2048]{1,0:T(8,128)}), f32[1024,128]{1,0:T(8,128)}) %reduce-scatter.17.cloned.1.call-update) | async-done | bytes 524304 | tf_op jit(solution)/shard_map/reduce_scatter | solution.py:267
  906.0 247.5 %reduce-scatter.15.cloned.1.call-done = f32[3,128,1024]{2,1,0:T(8,128)} async-done(((f32[3,2048,1024]{2,1,0:T(8,128)}), f32[3,128,1024]{2,1,0:T(8,128)}) %reduce-scatter.15.cloned.1.call-update) | async-done | bytes 1572880 | tf_op jit(solution)/shard_map/reduce_scatter | solution.py:265
  1153.6 334.5 %reduce-scatter.19.cloned.1.call-done = f32[128,4096]{1,0:T(8,128)} async-done(((f32[2048,4096]{1,0:T(8,128)}), f32[128,4096]{1,0:T(8,128)}) %reduce-scatter.19.cloned.1.call-update) | async-done | bytes 2097168 | tf_op jit(solution)/shard_map/reduce_scatter | solution.py:269
  1488.1 334.1 %reduce-scatter.21.cloned.1.call-done = f32[4096,128]{1,0:T(8,128)} async-done(((f32[4096,2048]{1,0:T(8,128)}), f32[4096,128]{1,0:T(8,128)}) %reduce-scatter.21.cloned.1.call-update) | async-done | bytes 2097168 | tf_op jit(solution)/shard_map/reduce_scatter | solution.py:271
  (220 shorter events, 145.3 us)
Async XLA Ops:
  7.2 48.3 %copy-start.30 = (bf16[32,8]{0,1:T(8,128)(2,1)S(1)}, bf16[32,8]{0,1:T(8,128)(2,1)}, u32[]{:S(2)}) copy-start(bf16[32,8]{0,1:T(8,128)(2,1)} %param.21) | copy-start | bytes 1540
  7.2 70.4 %copy-start.31 = (bf16[2,128]{1,0:T(2,128)(2,1)S(1)}, bf16[2,128]{1,0:T(2,128)(2,1)}, u32[]{:S(2)}) copy-start(bf16[2,128]{1,0:T(2,128)(2,1)} %param.14) | copy-start | bytes 1540
  7.2 322.1 %all-gather.9.cloned.1.call-start = ((), (), s32[]{:S(2)}) async-start(), calls=%async_computation.8 | async-start | bytes 4456448 | tf_op jit(solution)/shard_map/all_gather | solution.py:162
  7.9 330.0 %all-gather.7.cloned.1.call-start = ((), (), s32[]{:S(2)}) async-start(), calls=%async_computation.7 | async-start | bytes 13369344 | tf_op jit(solution)/shard_map/all_gather | solution.py:160
  8.7 384.3 %all-gather.11.cloned.1.call-start = ((), (), s32[]{:S(2)}) async-start(), calls=%async_computation.9 | async-start | bytes 17825792 | tf_op jit(solution)/shard_map/all_gather | solution.py:164
  9.4 501.9 %all-gather.13.cloned.1.call-start = ((), (), s32[]{:S(2)}) async-start(), calls=%async_computation.10 | async-start | bytes 17825792 | tf_op jit(solution)/shard_map/all_gather | solution.py:205
  10.0 608.5 %all-reduce.6.cloned.1.call-start = ((), (), s32[]{:S(2)}) async-start(), calls=%async_computation.18 | async-start | bytes 6291456 | tf_op jit(solution)/shard_map/psum | solution.py:198
  10.0 66.7 %collective-permute-start = (bf16[4096,128]{1,0:T(8,128)(2,1)}, bf16[4096,128]{1,0:T(8,128)(2,1)S(1)}, u32[]{:S(2)}, u32[]{:S(2)}) collective-permute-start(bf16[4096,128]{1,0:T(8,128)(2,1)} %param.22), channel_id=1, source_target_pairs={{0,2},{2,4},{4,6},{6,8},{8,10},{10,12},{12,14},{14,16},{16,18},{18... | collective-permute-start | bytes 3145736 | tf_op jit(solution)/shard_map/ppermute | solution.py:24
  10.6 100.9 %collective-permute-start.1 = (bf16[4096,128]{1,0:T(8,128)(2,1)}, bf16[4096,128]{1,0:T(8,128)(2,1)S(1)}, u32[]{:S(2)}, u32[]{:S(2)}) collective-permute-start(bf16[4096,128]{1,0:T(8,128)(2,1)} %param.22), channel_id=1, source_target_pairs={{0,30},{2,0},{4,2},{6,4},{8,6},{10,8},{12,10},{14,12},{16,14},{18,... | collective-permute-start | bytes 3145736 | tf_op jit(solution)/shard_map/ppermute | solution.py:29
  55.4 55.6 %copy-start.21 = (f32[256]{0:T(256)}, f32[256]{0:T(256)S(1)}, u32[]{:S(2)}) copy-start(f32[256]{0:T(256)S(1)} %broadcast_multiply_fusion.3) | copy-start | bytes 3076
  76.8 36.3 %collective-permute-start.2 = (bf16[4096,128]{1,0:T(8,128)(2,1)S(1)}, bf16[4096,128]{1,0:T(8,128)(2,1)}, u32[]{:S(2)}, u32[]{:S(2)}) collective-permute-start(bf16[4096,128]{1,0:T(8,128)(2,1)S(1)} %collective-permute-done), channel_id=1, source_target_pairs={{0,2},{2,4},{4,6},{6,8},{8,10},{10,12},{12,14},{14,16},{16,18},{18... | collective-permute-start | bytes 3145736 | tf_op jit(solution)/shard_map/ppermute | solution.py:24
  111.5 58.4 %collective-permute-start.3 = (bf16[4096,128]{1,0:T(8,128)(2,1)S(1)}, bf16[4096,128]{1,0:T(8,128)(2,1)}, u32[]{:S(2)}, u32[]{:S(2)}) collective-permute-start(bf16[4096,128]{1,0:T(8,128)(2,1)S(1)} %collective-permute-done.1), channel_id=1, source_target_pairs={{0,30},{2,0},{4,2},{6,4},{8,6},{10,8},{12,10},{14,12},{16,14},{18,... | collective-permute-start | bytes 3145736 | tf_op jit(solution)/shard_map/ppermute | solution.py:29
  113.1 64.7 %collective-permute-start.4 = (bf16[4096,128]{1,0:T(8,128)(2,1)}, bf16[4096,128]{1,0:T(8,128)(2,1)}, u32[]{:S(2)}, u32[]{:S(2)}) collective-permute-start(bf16[4096,128]{1,0:T(8,128)(2,1)} %collective-permute-done.2), channel_id=1, source_target_pairs={{0,2},{2,4},{4,6},{6,8},{8,10},{10,12},{12,14},{14,16},{16,18},{18... | collective-permute-start | bytes 3145736 | tf_op jit(solution)/shard_map/ppermute | solution.py:24
  169.9 29.5 %collective-permute-start.5 = (bf16[4096,128]{1,0:T(8,128)(2,1)}, bf16[4096,128]{1,0:T(8,128)(2,1)S(1)}, u32[]{:S(2)}, u32[]{:S(2)}) collective-permute-start(bf16[4096,128]{1,0:T(8,128)(2,1)} %collective-permute-done.3), channel_id=1, source_target_pairs={{0,30},{2,0},{4,2},{6,4},{8,6},{10,8},{12,10},{14,12},{16,14},{18,... | collective-permute-start | bytes 3145736 | tf_op jit(solution)/shard_map/ppermute | solution.py:29
  177.8 29.7 %collective-permute-start.6 = (bf16[4096,128]{1,0:T(8,128)(2,1)}, bf16[4096,128]{1,0:T(8,128)(2,1)S(1)}, u32[]{:S(2)}, u32[]{:S(2)}) collective-permute-start(bf16[4096,128]{1,0:T(8,128)(2,1)} %collective-permute-done.4), channel_id=1, source_target_pairs={{0,2},{2,4},{4,6},{6,8},{8,10},{10,12},{12,14},{14,16},{16,18},{18... | collective-permute-start | bytes 3145736 | tf_op jit(solution)/shard_map/ppermute | solution.py:24
  199.5 27.9 %collective-permute-start.7 = (bf16[4096,128]{1,0:T(8,128)(2,1)S(1)}, bf16[4096,128]{1,0:T(8,128)(2,1)S(1)}, u32[]{:S(2)}, u32[]{:S(2)}) collective-permute-start(bf16[4096,128]{1,0:T(8,128)(2,1)S(1)} %collective-permute-done.5), channel_id=1, source_target_pairs={{0,30},{2,0},{4,2},{6,4},{8,6},{10,8},{12,10},{14,12},{16,14},{18,... | collective-permute-start | bytes 3145736 | tf_op jit(solution)/shard_map/ppermute | solution.py:29
  207.4 34.3 %collective-permute-start.8 = (bf16[4096,128]{1,0:T(8,128)(2,1)S(1)}, bf16[4096,128]{1,0:T(8,128)(2,1)S(1)}, u32[]{:S(2)}, u32[]{:S(2)}) collective-permute-start(bf16[4096,128]{1,0:T(8,128)(2,1)S(1)} %collective-permute-done.6), channel_id=1, source_target_pairs={{0,2},{2,4},{4,6},{6,8},{8,10},{10,12},{12,14},{14,16},{16,18},{18... | collective-permute-start | bytes 3145736 | tf_op jit(solution)/shard_map/ppermute | solution.py:24
  227.3 33.3 %collective-permute-start.9 = (bf16[4096,128]{1,0:T(8,128)(2,1)S(1)}, bf16[4096,128]{1,0:T(8,128)(2,1)S(1)}, u32[]{:S(2)}, u32[]{:S(2)}) collective-permute-start(bf16[4096,128]{1,0:T(8,128)(2,1)S(1)} %collective-permute-done.7), channel_id=1, source_target_pairs={{0,30},{2,0},{4,2},{6,4},{8,6},{10,8},{12,10},{14,12},{16,14},{18,... | collective-permute-start | bytes 3145736 | tf_op jit(solution)/shard_map/ppermute | solution.py:29
  241.8 27.8 %collective-permute-start.10 = (bf16[4096,128]{1,0:T(8,128)(2,1)S(1)}, bf16[4096,128]{1,0:T(8,128)(2,1)S(1)}, u32[]{:S(2)}, u32[]{:S(2)}) collective-permute-start(bf16[4096,128]{1,0:T(8,128)(2,1)S(1)} %collective-permute-done.8), channel_id=1, source_target_pairs={{0,2},{2,4},{4,6},{6,8},{8,10},{10,12},{12,14},{14,16},{16,18},{18... | collective-permute-start | bytes 3145736 | tf_op jit(solution)/shard_map/ppermute | solution.py:24
  260.6 36.1 %collective-permute-start.11 = (bf16[4096,128]{1,0:T(8,128)(2,1)S(1)}, bf16[4096,128]{1,0:T(8,128)(2,1)S(1)}, u32[]{:S(2)}, u32[]{:S(2)}) collective-permute-start(bf16[4096,128]{1,0:T(8,128)(2,1)S(1)} %collective-permute-done.9), channel_id=1, source_target_pairs={{0,30},{2,0},{4,2},{6,4},{8,6},{10,8},{12,10},{14,12},{16,14},{18,... | collective-permute-start | bytes 3145736 | tf_op jit(solution)/shard_map/ppermute | solution.py:29
  269.6 39.5 %collective-permute-start.12 = (bf16[4096,128]{1,0:T(8,128)(2,1)S(1)}, bf16[4096,128]{1,0:T(8,128)(2,1)S(1)}, u32[]{:S(2)}, u32[]{:S(2)}) collective-permute-start(bf16[4096,128]{1,0:T(8,128)(2,1)S(1)} %collective-permute-done.10), channel_id=1, source_target_pairs={{0,2},{2,4},{4,6},{6,8},{8,10},{10,12},{12,14},{14,16},{16,18},{18... | collective-permute-start | bytes 3145736 | tf_op jit(solution)/shard_map/ppermute | solution.py:24
  270.7 58.6 %copy-start.1 = (bf16[256,2048]{1,0:T(8,128)(2,1)S(1)}, bf16[256,2048]{1,0:T(8,128)(2,1)}, u32[]{:S(2)}) copy-start(bf16[256,2048]{1,0:T(8,128)(2,1)} %param.13) | copy-start | bytes 3145732
  296.7 31.5 %collective-permute-start.13 = (bf16[4096,128]{1,0:T(8,128)(2,1)S(1)}, bf16[4096,128]{1,0:T(8,128)(2,1)S(1)}, u32[]{:S(2)}, u32[]{:S(2)}) collective-permute-start(bf16[4096,128]{1,0:T(8,128)(2,1)S(1)} %collective-permute-done.11), channel_id=1, source_target_pairs={{0,30},{2,0},{4,2},{6,4},{8,6},{10,8},{12,10},{14,12},{16,14},{18,... | collective-permute-start | bytes 3145736 | tf_op jit(solution)/shard_map/ppermute | solution.py:29
  309.1 26.5 %collective-permute-start.14 = (bf16[4096,128]{1,0:T(8,128)(2,1)S(1)}, bf16[4096,128]{1,0:T(8,128)(2,1)}, u32[]{:S(2)}, u32[]{:S(2)}) collective-permute-start(bf16[4096,128]{1,0:T(8,128)(2,1)S(1)} %collective-permute-done.12), channel_id=1, source_target_pairs={{0,2},{2,4},{4,6},{6,8},{8,10},{10,12},{12,14},{14,16},{16,18},{18... | collective-permute-start | bytes 3145736 | tf_op jit(solution)/shard_map/ppermute | solution.py:24
  534.4 180.2 %reduce-scatter.27.cloned.1.call-start = ((), (), s32[]{:S(2)}) async-start(), calls=%async_computation.17 | async-start | bytes 139264
  538.6 85.9 %copy-start.14 = (bf16[4,256,256]{2,1,0:T(8,128)(2,1)S(1)}, bf16[4,256,256]{2,1,0:T(8,128)(2,1)}, u32[]{:S(2)}) copy-start(bf16[4,256,256]{2,1,0:T(8,128)(2,1)} %copy-done.13) | copy-start | bytes 1572868
  539.6 242.2 %reduce-scatter.25.cloned.1.call-start = ((), (), s32[]{:S(2)}) async-start(), calls=%async_computation.16 | async-start | bytes 1114112
  623.1 175.7 %reduce-scatter.23.cloned.1.call-start = ((), (), s32[]{:S(2)}) async-start(), calls=%async_computation.15 | async-start | bytes 1114112
  624.5 281.5 %reduce-scatter.17.cloned.1.call-start = ((), (), s32[]{:S(2)}) async-start(), calls=%async_computation.12 | async-start | bytes 8912896 | tf_op jit(solution)/shard_map/reduce_scatter | solution.py:267
  629.2 524.4 %reduce-scatter.15.cloned.1.call-start = ((), (), s32[]{:S(2)}) async-start(), calls=%async_computation.11 | async-start | bytes 26738688 | tf_op jit(solution)/shard_map/reduce_scatter | solution.py:265
  643.3 844.8 %reduce-scatter.19.cloned.1.call-start = ((), (), s32[]{:S(2)}) async-start(), calls=%async_computation.13 | async-start | bytes 35651584 | tf_op jit(solution)/shard_map/reduce_scatter | solution.py:269
  658.3 1163.9 %reduce-scatter.21.cloned.1.call-start = ((), (), s32[]{:S(2)}) async-start(), calls=%async_computation.14 | async-start | bytes 35651584 | tf_op jit(solution)/shard_map/reduce_scatter | solution.py:271
  (32 other events, 264.0 us)
Sparse Core Ops, SparseCore 0:
  10.2 64.9 all-gather.8
  77.3 120.4 all-gather.6
  200.0 175.0 all-gather.10
  377.0 134.2 all-gather.12
  534.5 84.0 all-reduce.5
  622.4 55.5 reduce-scatter.26
  681.7 56.6 reduce-scatter.24
  742.0 56.7 reduce-scatter.22
  803.4 102.5 reduce-scatter.16
  910.6 242.9 reduce-scatter.14
  1158.4 329.6 reduce-scatter.18
  1492.7 329.4 reduce-scatter.20
